TPU v7x, 32 devices: a whole 2x2x4 slice. The times are simulated.
32 devices in a mesh: store: 8 (over y, x, core), vocab: 4 (over z).
Axes of the slice: x: 2, y: 2, z: 4, core: 2. Of those that a mesh axis runs over, the one named last changes fastest.
Arguments:
- hidden: bfloat16 [512, 4096], P('store')
- lm_head: bfloat16 [4096, 65536], P(None, ('store', 'vocab'))
- store_keys: bfloat16 [8192, 4096], P(('store', 'vocab'))
- values: int32 [8192], P(('store', 'vocab')), may hold values from 0 to 65535, as said below
- licences: int32 [8192], P(('store', 'vocab')), may hold values from 0 to 29, as said below
- allowed: int32 [512], replicated, may hold values from 1 to 1073741823, as said below
Outputs:
- log_probs: float32 [512, 65536], P(None, ('store', 'vocab'))
Inputs may be any that keep to these rules, and one draw needn't show every extreme that they name: `values`: entry i holds a token t with t // 2048 = (i // 1024) * 4 + (i // 64) % 4: the entries of a device name tokens of the 8192 columns of its index along store, and its k-th run of 64 entries names tokens of the k-th 2048 columns of those. `licences`: some entry has licence 0. `allowed`: bit l of a position's word says whether licence l may be used; bit 0 is always set.
All inputs are finite; a program needn't handle non-finite values.
Results may differ from a plain program's by a relative error of at most 0.0003.
Values may be sent and summed in bfloat16 or wider, within the bound.
A program may use at most 128 MiB of HBM per device.

v0:
```python
import math

import jax
import jax.numpy as jnp
from jax import lax
from jax.sharding import PartitionSpec as P

NEG_FILL = -1e30


def mixture(lm_log, knn_mass, knn_total):
    share = knn_mass / knn_total[:, None]
    present = share > 0.0
    knn_log = jnp.where(present, jnp.log(jnp.where(present, share, 1.0)), -jnp.inf)
    return jnp.logaddexp(math.log(0.75) + lm_log, math.log(0.25) + knn_log)


def bin_tokens(weights, tokens, first_col, width):
    columns = lax.broadcasted_iota(jnp.int32, (tokens.shape[0], width), 1)
    token_table = ((tokens - first_col)[:, None] == columns).astype(jnp.float32)
    return jnp.dot(
        weights, token_table, precision=lax.Precision.HIGHEST, preferred_element_type=jnp.float32
    )


def body(hidden, lm_head, store_keys, values, licences, allowed):
    own_cols = lm_head.shape[1]
    inverse_root = 1.0 / math.sqrt(store_keys.shape[1])
    wide_keys = store_keys.astype(jnp.float32)
    key_half = 0.5 * jnp.sum(wide_keys * wide_keys, axis=1) * inverse_root
    portion = lax.all_gather(hidden, "store", axis=0, tiled=True)
    logit_rows = jnp.dot(portion, lm_head, preferred_element_type=jnp.float32)
    score_rows = lax.dot_general(
        portion, store_keys, (((1,), (1,)), ((), ())), preferred_element_type=jnp.float32
    )
    joined = jnp.concatenate([logit_rows, score_rows * inverse_root - key_half[None, :]], axis=1)
    logits = joined[:, :own_cols]
    scores = joined[:, own_cols:]
    permitted = jnp.bitwise_and(jnp.right_shift(allowed[:, None], licences[None, :]), 1) == 1
    masked = jnp.where(permitted, scores, NEG_FILL)
    lm_max, knn_max = lax.pmax(
        (jnp.max(logits, axis=1), jnp.max(masked, axis=1)), ("store", "vocab")
    )
    lm_terms = jnp.exp(logits - lm_max[:, None])
    kernel = jnp.where(permitted, jnp.exp(masked - knn_max[:, None]), 0.0)
    lm_total, knn_total = lax.psum(
        (jnp.sum(lm_terms, axis=1), jnp.sum(kernel, axis=1)), ("store", "vocab")
    )
    lm_log = logits - lm_max[:, None] - jnp.log(lm_total)[:, None]
    received, sources = (
        lax.all_to_all(
            kernel.astype(jnp.bfloat16), "vocab", split_axis=1, concat_axis=1, tiled=True
        ).astype(kernel.dtype),
        lax.all_to_all(values[None, :], "vocab", split_axis=1, concat_axis=1, tiled=True),
    )
    first_col = (
        lax.axis_index("store") * lax.axis_size("vocab") + lax.axis_index("vocab")
    ) * own_cols
    knn_mass = bin_tokens(received, sources[0], first_col, own_cols)
    return mixture(lm_log, knn_mass, knn_total)


def solution(mesh):
    return jax.shard_map(
        body,
        mesh=mesh,
        in_specs=(
            P("store", None),
            P(None, ("store", "vocab")),
            P(("store", "vocab"), None),
            P(("store", "vocab")),
            P(("store", "vocab")),
            P(),
        ),
        out_specs=P(None, ("store", "vocab")),
        check_vma=False,
    )
```

profile of v0, /device:TPU:0, one launch (start us, length us, event | category | flops | bytes accessed | tf_op | source)
XLA Modules:
  0.0 170.6 jit_solution(7530144514574135348)
XLA Ops:
  6.5 0.0 all-gather.2.cloned.1.call-start
  6.5 0.7 all-gather.2.cloned.1.call-update
  7.3 1.3 all_to_all.17
  8.6 6.3 %all-to-all-start.1 = ((s32[1,4,64]{2,0,1:T(1,128)}), s32[1,4,64]{2,0,1:T(1,128)S(1)}, u32[]{:S(2)}, u32[]{:S(2)}) async-start(s32[1,4,64]{2,0,1:T(1,128)} %all_to_all.17), calls=%async_computation.1 | async-start | bytes 4096 | tf_op jit(solution)/shard_map/all_to_all | solution.py:54
  14.9 2.1 %multiply_reduce_fusion = f32[256]{0:T(256)S(1)} fusion(bf16[256,4096]{1,0:T(8,128)(2,1)} %param.8), kind=kLoop, calls=%fused_computation.5 | loop fusion | flops 3145472 | bytes 2098176 | tf_op jit(solution)/shard_map/reduce_sum | solution.py:30
  17.0 0.0 copy-start
  17.0 0.0 copy-start.1
  17.0 0.0 copy-start.2
  17.0 31.7 %all-gather.2.cloned.1.call-done = bf16[512,4096]{1,0:T(8,128)(2,1)} async-done(((bf16[64,4096]{1,0:T(8,128)(2,1)}), bf16[512,4096]{1,0:T(8,128)(2,1)}) %all-gather.2.cloned.1.call-update) | async-done | bytes 4194320 | tf_op jit(solution)/shard_map/all_gather | solution.py:31
  48.7 0.0 copy-start.3
  48.7 17.1 %fusion.8 = (f32[512]{0:T(512)S(1)}, f32[512,2048]{1,0:T(8,128)}) fusion(bf16[512,4096]{1,0:T(8,128)(2,1)} %all-gather.2.cloned.1.call-done, bf16[4096,2048]{1,0:T(8,128)(2,1)} %param.7), kind=kOutput, calls=%fused_computation.20 | convolution fusion | flops 8590983168 | bytes 25167872 | tf_op jit(solution)/shard_map/dot_general | solution.py:32
  65.8 0.0 copy-done
  65.8 0.0 copy-done.1
  65.8 0.0 copy-done.2
  65.8 0.0 copy-done.3
  65.8 1.3 fusion.7
  67.1 39.4 %all-reduce.1 = (f32[512]{0:T(512)S(1)}, f32[512]{0:T(512)S(1)}) all-reduce(f32[512]{0:T(512)S(1)} %get-tuple-element.11, f32[512]{0:T(512)S(1)} %get-tuple-element.13), channel_id=1, replica_groups=mesh['store'=8,'vocab'=4] {'store','vocab'}, use_global_device_ids=true, to_apply=%region_6.7 | all-reduce | flops 1024 | bytes 8192 | tf_op jit(solution)/shard_map/pmax | solution.py:41
  106.5 0.9 fusion.5
  107.3 0.0 all-to-all-done.1
  107.3 3.6 %all-to-all-start = ((bf16[512,4,64]{0,2,1:T(8,128)(2,1)}), bf16[512,4,64]{0,2,1:T(8,128)(2,1)S(1)}, u32[]{:S(2)}, u32[]{:S(2)}) async-start(bf16[512,4,64]{0,2,1:T(8,128)(2,1)} %bitcast), calls=%async_computation | async-start | bytes 524288 | tf_op jit(solution)/shard_map/all_to_all | solution.py:51
  110.9 0.1 sub.62
  111.0 2.9 %exponential_reduce_fusion = f32[512]{0:T(512)S(1)} fusion(f32[512,2048]{1,0:T(8,128)} %get-tuple-element.14, f32[512]{0:T(512)S(1)} %get-tuple-element.8), kind=kLoop, calls=%fused_computation.7 | loop fusion | flops 2096640 | bytes 4198400 | tf_op jit(solution)/shard_map/reduce_sum | solution.py:47
  113.9 41.6 %all-reduce = (f32[512]{0:T(512)S(1)}, f32[512]{0:T(512)S(1)}) all-reduce(f32[512]{0:T(512)S(1)} %get-tuple-element.9, f32[512]{0:T(512)S(1)} %exponential_reduce_fusion), channel_id=1, replica_groups=mesh['store'=8,'vocab'=4] {'store','vocab'}, use_global_device_ids=true, to_apply=%region_8.9 | all-reduce | flops 1024 | bytes 8192 | tf_op jit(solution)/shard_map/psum | solution.py:46
  155.5 0.0 all-to-all-done
  155.5 8.2 %add_select_fusion = f32[512,2048]{1,0:T(8,128)} fusion(f32[512,2048]{1,0:T(8,128)} %get-tuple-element.14, bf16[512,256]{0,1:T(8,128)(2,1)S(1)} %bitcast.7, f32[512]{0:T(512)S(1)} %get-tuple-element.5, f32[512]{0:T(512)S(1)} %log.6, f32[512]{0:T(512)S(1)} %get-tuple-element.8, s32[256]{0:T(256)S(1)} %sub.62), kind=kOutput, calls=%fused_computation.4 | convolution fusion | flops 554172416 | bytes 8657920 | tf_op jit(solution)/shard_map/dot_general | solution.py:21
  (3 shorter events, 0.0 us)
Async XLA Ops:
  6.5 42.2 %all-gather.2.cloned.1.call-start = ((), (), s32[]{:S(2)}) async-start(), calls=%async_computation.2 | async-start | bytes 4718592 | tf_op jit(solution)/shard_map/all_gather | solution.py:31
  8.6 98.7 %all-to-all-start.1 = ((s32[1,4,64]{2,0,1:T(1,128)}), s32[1,4,64]{2,0,1:T(1,128)S(1)}, u32[]{:S(2)}, u32[]{:S(2)}) async-start(s32[1,4,64]{2,0,1:T(1,128)} %all_to_all.17), calls=%async_computation.1 | async-start | bytes 4096 | tf_op jit(solution)/shard_map/all_to_all | solution.py:54
  17.0 48.8 %copy-start = (bf16[256,4096]{1,0:T(8,128)(2,1)S(1)}, bf16[256,4096]{1,0:T(8,128)(2,1)}, u32[]{:S(2)}) copy-start(bf16[256,4096]{1,0:T(8,128)(2,1)} %param.8) | copy-start | bytes 6291460
  17.0 48.7 %copy-start.1 = (s32[512]{0:T(512)S(1)}, s32[512]{0:T(512)}, u32[]{:S(2)}) copy-start(s32[512]{0:T(512)} %param.11) | copy-start | bytes 6148
  17.0 48.7 %copy-start.2 = (s32[256]{0:T(256)S(1)}, s32[256]{0:T(256)}, u32[]{:S(2)}) copy-start(s32[256]{0:T(256)} %param.10) | copy-start | bytes 3076
  48.7 17.1 %copy-start.3 = (bf16[512,4096]{1,0:T(8,128)(2,1)S(1)}, bf16[512,4096]{1,0:T(8,128)(2,1)}, u32[]{:S(2)}) copy-start(bf16[512,4096]{1,0:T(8,128)(2,1)} %all-gather.2.cloned.1.call-done) | copy-start | bytes 12582916
  107.3 48.2 %all-to-all-start = ((bf16[512,4,64]{0,2,1:T(8,128)(2,1)}), bf16[512,4,64]{0,2,1:T(8,128)(2,1)S(1)}, u32[]{:S(2)}, u32[]{:S(2)}) async-start(bf16[512,4,64]{0,2,1:T(8,128)(2,1)} %bitcast), calls=%async_computation | async-start | bytes 524288 | tf_op jit(solution)/shard_map/all_to_all | solution.py:51
Sparse Core Ops, SparseCore 0:
  9.2 39.4 all-gather.1
where the time goes:
time: 171 us
  blocking collectives  81 us (47%)
  waiting for transfers between devices  32.4 us (19%)
  matrix products  26.6 us (16%)
  between operations  13.4 us (8%)
  starting transfers between devices  9.87 us (6%)
  other arithmetic  5.86 us (3%)
    psum x1, blocking collectives, body(): lax.psum((jnp.sum(lm_terms, axis=1), jnp.sum(kernel, axis=1)), ('store',...  41.6 us
    pmax x1, blocking collectives, body(): lax.pmax((jnp.max(logits, axis=1), jnp.max(masked, axis=1)), ('store', 'v...  39.4 us
    all_gather x1, waiting for transfers between devices, body(): portion = lax.all_gather(hidden, 'store', axis=0, tiled=True)  31.7 us
    dot_general x1, matrix products, body(): logit_rows = jnp.dot(portion, lm_head, preferred_element_type=jnp.float32)  17.1 us
    dot_general x1, matrix products, bin_tokens(): jnp.dot(weights, token_table, precision=lax.Precision.HIGHEST, preferred_...  8.19 us
    all_to_all x1, starting transfers between devices, body(): lax.all_to_all(values[None, :], 'vocab', split_axis=1, concat_axis=1, til...  6.32 us
    all_to_all x1, starting transfers between devices, body(): lax.all_to_all(kernel.astype(jnp.bfloat16), 'vocab', split_axis=1, concat...  3.55 us
  transfers between devices with their start and end apart: 3, of which 1 were waited for; matrix products, arithmetic and copies ran while one was open for 14% of the time, Pallas kernels for 0%

commit v1 on v0

v1 whole, which is shorter than its diff:
```python
import functools
import math

import jax
import jax.numpy as jnp
from jax import lax
from jax.experimental import pallas as pl
from jax.experimental.pallas import tpu as pltpu
from jax.sharding import PartitionSpec as P

NEG_FILL = -1e30
DEPTH_CHUNK = 512
MESH = pl.DeviceIdType.MESH


def row_to_column(row, lanes=128):
    return jnp.broadcast_to(row, (lanes, row.shape[1])).T


def gather_kernel(
    S, V,
    hidden, lm_head, keys, values, licences, allowed,
    logits_out, weights_out, tokens_out, shift_out,
    hid, head, key, logits, scores, half, wsend, wrecv, tok, tokcol, turn, stat, st1, st1_all, st2, st2_all,
    own_sem, head_sem, key_sem, out_sem, gsend, grecv, tsend, trecv, wsend_sem, wrecv_sem,
    s1send, s1recv, s2send, s2recv,
):
    R, D = hidden.shape
    C = lm_head.shape[1]
    E = keys.shape[0]
    Q = hid.shape[1]
    K, KC = hid.shape[0], hid.shape[2]
    B = E // V
    inverse_root = 1.0 / math.sqrt(D)
    s = lax.axis_index("store")
    v = lax.axis_index("vocab")

    def rows(origin):
        return pl.ds(pl.multiple_of(origin * R, R), R)

    def remote(src, dst, send, recv, store, vocab):
        return pltpu.make_async_remote_copy(
            src_ref=src, dst_ref=dst, send_sem=send, recv_sem=recv,
            device_id=(store, vocab), device_id_type=MESH,
        )

    def own_copy(k):
        return pltpu.make_async_copy(
            hidden.at[:, pl.ds(pl.multiple_of(k * KC, KC), KC)], hid.at[k, rows(s)], own_sem.at[k]
        )

    def head_copy(k):
        return pltpu.make_async_copy(
            lm_head.at[pl.ds(pl.multiple_of(k * KC, KC), KC)], head.at[k], head_sem.at[k]
        )

    def key_copy(k):
        return pltpu.make_async_copy(
            keys.at[:, pl.ds(pl.multiple_of(k * KC, KC), KC)], key.at[k], key_sem.at[k]
        )

    def loop_all(f):
        def step(k, carry):
            f(k)
            return carry
        lax.fori_loop(0, K, step, 0)

    loop_all(lambda k: own_copy(k).start())
    loop_all(lambda k: key_copy(k).start())
    tok[...] = jnp.broadcast_to(values[...], tok.shape)

    store_peers = [lax.rem(s + j, S) for j in range(1, S)]
    vocab_peers = [lax.rem(v + j, V) for j in range(1, V)]
    vocab_from = [lax.rem(v + V - j, V) for j in range(1, V)]
    store_from = [lax.rem(s + S - j, S) for j in range(1, S)]

    barrier = pltpu.get_barrier_semaphore()
    for peer in store_peers:
        pl.semaphore_signal(barrier, inc=1, device_id=(peer, v), device_id_type=MESH)
    for peer in vocab_peers:
        pl.semaphore_signal(barrier, inc=1, device_id=(s, peer), device_id_type=MESH)
    pl.semaphore_wait(barrier, S + V - 2)

    tuned = S == 8 and V % 2 == 0
    if tuned:
        odd = lax.rem(v, 2)
        along_x = 2 - 4 * lax.rem(lax.div(s, 2), 2)
        along_y = 4 - 8 * lax.rem(lax.div(s, 4), 2)
        first = s + along_x * (1 - odd) + along_y * odd
        second = s + along_y * (1 - odd) + along_x * odd
        diagonal = s + along_x + along_y
        across = 1 - 2 * lax.rem(s, 2)
        pair = v + 1 - 2 * odd
        streams = [
            (s, (first, v), first),
            (first, (second, v), diagonal),
            (first, (s, pair), second),
            (s, (s + across, v), s + across),
            (first, (s + across, v), first + across),
            (diagonal, (s + across, v), diagonal + across),
            (second, (s + across, v), second + across),
        ]
    else:
        streams = [(s, (peer, v), source) for peer, source in zip(store_peers, store_from)]

    def send(t, k):
        origin, target, _ = streams[t]
        if origin is s:
            src = hidden.at[:, pl.ds(pl.multiple_of(k * KC, KC), KC)]
        else:
            src = hid.at[k, rows(origin)]
        return remote(src, hid.at[k, rows(origin)], gsend.at[t, k], grecv.at[t, k], *target)

    def arrive(t, k):
        _, target, origin = streams[t]
        block = hid.at[k, rows(origin)]
        return remote(block, block, gsend.at[t, k], grecv.at[t, k], *target)

    if tuned:
        loop_all(lambda k: send(0, k).start())
        loop_all(lambda k: send(3, k).start())
    else:
        for t in range(len(streams)):
            loop_all(lambda k: send(t, k).start())
    loop_all(lambda k: head_copy(k).start())

    token_sends = []
    for j in range(1, V):
        copy = remote(tok, tokcol.at[v], tsend.at[j - 1], trecv.at[j - 1], s, vocab_peers[j - 1])
        copy.start()
        token_sends.append(copy)
    tokcol[v] = tok[...]

    logits[...] = jnp.zeros_like(logits)
    scores[...] = jnp.zeros_like(scores)
    half[...] = jnp.zeros_like(half)

    def norm_step(k, carry):
        key_copy(k).wait()
        wide = key[k].astype(jnp.float32)
        half[...] += jnp.sum(wide * wide, axis=1, keepdims=True)
        return carry

    lax.fori_loop(0, K, norm_step, 0)

    NT = math.gcd(C, 256)

    def compute(k):
        own_copy(k).wait()
        scores[...] += lax.dot_general(
            key[k], hid[k], (((1,), (1,)), ((), ())), preferred_element_type=jnp.float32
        )
        head_copy(k).wait()

        def column_step(n, carry):
            cols = pl.ds(pl.multiple_of(n * NT, NT), NT)
            logits[:, cols] += jnp.dot(
                hid[k], head[k, :, cols], preferred_element_type=jnp.float32
            )
            return carry

        lax.fori_loop(0, C // NT, column_step, 0)

    if tuned:
        def gather_step(k, carry):
            @pl.when(k < K)
            def _():
                arrive(0, k).wait_recv()
                send(1, k).start()
                send(2, k).start()
                send(4, k).start()

            @pl.when(jnp.logical_and(k >= 1, k <= K))
            def _():
                arrive(1, k - 1).wait_recv()
                send(5, k - 1).start()
                arrive(2, k - 1).wait_recv()
                send(6, k - 1).start()

            @pl.when(k >= 2)
            def _():
                for t in range(3, 7):
                    arrive(t, k - 2).wait_recv()
                compute(k - 2)

            return carry

        lax.fori_loop(0, K + 2, gather_step, 0)
    else:
        def gather_step(k, carry):
            for t in range(len(streams)):
                arrive(t, k).wait_recv()
            compute(k)
            return carry

        lax.fori_loop(0, K, gather_step, 0)

    out_copy = pltpu.make_async_copy(logits, logits_out, out_sem)
    out_copy.start()

    licence = row_to_column(licences[...])[:, 0:1]
    permitted = jnp.bitwise_and(
        jnp.right_shift(
            jnp.broadcast_to(allowed[...], (E, Q)), jnp.broadcast_to(licence, (E, Q))
        ), 1) == 1
    masked = jnp.where(
        permitted, scores[...] * inverse_root - (0.5 * inverse_root) * half[...], NEG_FILL
    )
    near = jnp.max(masked, axis=0, keepdims=True)
    kernel = jnp.where(permitted, jnp.exp(masked - near), 0.0)
    mass = jnp.sum(kernel, axis=0, keepdims=True)
    wsend[...] = kernel.astype(jnp.bfloat16)
    weight_sends = []
    for j in range(1, V):
        peer = vocab_peers[j - 1]
        copy = remote(
            wsend.at[pl.ds(pl.multiple_of(peer * B, B), B)], wrecv.at[v],
            wsend_sem.at[j - 1], wrecv_sem.at[j - 1], s, peer,
        )
        copy.start()
        weight_sends.append(copy)
    wrecv[v] = wsend[pl.ds(pl.multiple_of(v * B, B), B), :]

    RT = math.gcd(Q, 64)
    lane = lax.broadcasted_iota(jnp.int32, (RT, 128), 1)

    def stat_step(r, carry):
        span = pl.ds(pl.multiple_of(r * RT, RT), RT)
        tile = logits[span, :]
        top = jnp.max(tile, axis=1, keepdims=True)
        total = jnp.sum(jnp.exp(tile - top), axis=1, keepdims=True)
        stat[span, :] = jnp.where(
            lane == 0, jnp.broadcast_to(top, (RT, 128)), jnp.broadcast_to(total, (RT, 128))
        )
        return carry

    lax.fori_loop(0, Q // RT, stat_step, 0)
    st1[0:2, :] = stat[...].T[0:2, :]
    st1[2:3, :] = near
    st1[3:4, :] = mass
    st1[4:8, :] = jnp.zeros((4, Q), jnp.float32)
    stat_sends = []
    for j in range(1, S):
        copy = remote(st1, st1_all.at[s], s1send.at[j - 1], s1recv.at[j - 1], store_peers[j - 1], v)
        copy.start()
        stat_sends.append(copy)
    st1_all[s] = st1[...]

    first_col = (s * V + v) * C
    for j in range(1, V):
        slot = tokcol.at[vocab_from[j - 1]]
        remote(slot, slot, tsend.at[j - 1], trecv.at[j - 1], s, vocab_peers[j - 1]).wait_recv()
    for u in range(V):
        turn[...] = row_to_column(tokcol[u, 0:1, :])
        tokens_out[u * B:(u + 1) * B, :] = turn[pl.ds(pl.multiple_of(v * B, B), B), :] - first_col

    def merge(ref, n):
        top = ref[0, 0:1, :]
        near_top = ref[0, 2:3, :]
        for i in range(1, n):
            top = jnp.maximum(top, ref[i, 0:1, :])
            near_top = jnp.maximum(near_top, ref[i, 2:3, :])
        total = jnp.zeros_like(top)
        near_total = jnp.zeros_like(top)
        for i in range(n):
            total += ref[i, 1:2, :] * jnp.exp(ref[i, 0:1, :] - top)
            near_total += ref[i, 3:4, :] * jnp.exp(ref[i, 2:3, :] - near_top)
        return top, total, near_top, near_total

    for j in range(1, S):
        slot = st1_all.at[store_from[j - 1]]
        remote(slot, slot, s1send.at[j - 1], s1recv.at[j - 1], store_peers[j - 1], v).wait_recv()
    for i, row in enumerate(merge(st1_all, S)):
        st2[i:i + 1, :] = row
    st2[4:5, :] = near
    st2[5:8, :] = jnp.zeros((3, Q), jnp.float32)
    for j in range(1, V):
        copy = remote(st2, st2_all.at[v], s2send.at[j - 1], s2recv.at[j - 1], s, vocab_peers[j - 1])
        copy.start()
        stat_sends.append(copy)
    st2_all[v] = st2[...]
    for j in range(1, V):
        source = vocab_from[j - 1]
        slot = st2_all.at[source]
        remote(slot, slot, s2send.at[j - 1], s2recv.at[j - 1], s, vocab_peers[j - 1]).wait_recv()
        slot = wrecv.at[source]
        remote(slot, slot, wsend_sem.at[j - 1], wrecv_sem.at[j - 1], s, vocab_peers[j - 1]).wait_recv()
    top, total, near_top, near_total = merge(st2_all, V)
    shift_out[...] = row_to_column(top + jnp.log(total) - math.log(0.75))
    for u in range(V):
        scale = 0.25 * jnp.exp(st2_all[u, 4:5, :] - near_top) / near_total
        weights_out[u * B:(u + 1) * B, :] = (wrecv[u].astype(jnp.float32) * scale).astype(jnp.bfloat16)

    if tuned:
        def drain(k):
            for t in range(len(streams)):
                send(t, k).wait_send()
        loop_all(drain)
    else:
        for t in range(len(streams)):
            loop_all(lambda k: send(t, k).wait_send())
    for copy in token_sends + weight_sends + stat_sends:
        copy.wait_send()
    out_copy.wait()


def mixture_kernel(weights, tokens, shift, logits, out):
    columns = lax.broadcasted_iota(jnp.int32, (tokens.shape[0], out.shape[1]), 1)
    columns += pl.program_id(0) * out.shape[1]
    table = jnp.where(tokens[:, 0:1] == columns, 1.0, 0.0).astype(jnp.bfloat16)
    share = lax.dot_general(
        weights[...], table, (((0,), (0,)), ((), ())), preferred_element_type=jnp.float32
    )
    ours = logits[...] - shift[:, 0:1]
    theirs = jnp.where(share > 0.0, jnp.log(jnp.where(share > 0.0, share, 1.0)), -jnp.inf)
    out[...] = jnp.maximum(ours, theirs) + jnp.log(1.0 + jnp.exp(-jnp.abs(ours - theirs)))


def body(S, V, hidden, lm_head, keys, values, licences, allowed):
    R, D = hidden.shape
    C = lm_head.shape[1]
    E = keys.shape[0]
    Q = allowed.shape[0]
    B = E // V
    KC = math.gcd(D, DEPTH_CHUNK)
    K = D // KC
    streams = S - 1
    any_space = pl.BlockSpec(memory_space=pl.ANY)
    vmem = pl.BlockSpec(memory_space=pltpu.VMEM)
    f32 = jnp.float32
    dma = pltpu.SemaphoreType.DMA
    logits, weights, tokens, shift = pl.pallas_call(
        functools.partial(gather_kernel, S, V),
        out_shape=(
            jax.ShapeDtypeStruct((Q, C), f32),
            jax.ShapeDtypeStruct((E, Q), jnp.bfloat16),
            jax.ShapeDtypeStruct((E, 128), jnp.int32),
            jax.ShapeDtypeStruct((Q, 128), f32),
        ),
        in_specs=[any_space] * 3 + [vmem] * 3,
        out_specs=(any_space, vmem, vmem, vmem),
        scratch_shapes=[
            pltpu.VMEM((K, Q, KC), hidden.dtype),
            pltpu.VMEM((K, KC, C), lm_head.dtype),
            pltpu.VMEM((K, E, KC), keys.dtype),
            pltpu.VMEM((Q, C), f32),
            pltpu.VMEM((E, Q), f32),
            pltpu.VMEM((E, 1), f32),
            pltpu.VMEM((E, Q), jnp.bfloat16),
            pltpu.VMEM((V, B, Q), jnp.bfloat16),
            pltpu.VMEM((8, E), jnp.int32),
            pltpu.VMEM((V, 8, E), jnp.int32),
            pltpu.VMEM((E, 128), jnp.int32),
            pltpu.VMEM((Q, 128), f32),
            pltpu.VMEM((8, Q), f32),
            pltpu.VMEM((S, 8, Q), f32),
            pltpu.VMEM((8, Q), f32),
            pltpu.VMEM((V, 8, Q), f32),
            dma((K,)), dma((K,)), dma((K,)), dma(()),
            dma((streams, K)), dma((streams, K)),
            dma((V - 1,)), dma((V - 1,)), dma((V - 1,)), dma((V - 1,)),
            dma((S - 1,)), dma((S - 1,)), dma((V - 1,)), dma((V - 1,)),
        ],
        compiler_params=pltpu.CompilerParams(
            collective_id=0, has_side_effects=True, vmem_limit_bytes=48 * 1024 * 1024
        ),
        name="gather_score",
    )(hidden, lm_head, keys, values.reshape(1, E), licences.reshape(1, E), allowed.reshape(1, Q))

    CT = math.gcd(C, 512)
    fixed = lambda shape: pl.BlockSpec(shape, lambda n: (0, 0))
    tile = pl.BlockSpec((Q, CT), lambda n: (0, n))
    return pl.pallas_call(
        mixture_kernel,
        grid=(C // CT,),
        out_shape=jax.ShapeDtypeStruct((Q, C), f32),
        in_specs=[fixed((E, Q)), fixed((E, 128)), fixed((Q, 128)), tile],
        out_specs=tile,
        compiler_params=pltpu.CompilerParams(vmem_limit_bytes=48 * 1024 * 1024),
        name="mixture",
    )(weights, tokens, shift, logits)


def solution(mesh):
    return jax.shard_map(
        functools.partial(body, mesh.shape["store"], mesh.shape["vocab"]),
        mesh=mesh,
        in_specs=(
            P("store", None),
            P(None, ("store", "vocab")),
            P(("store", "vocab"), None),
            P(("store", "vocab")),
            P(("store", "vocab")),
            P(),
        ),
        out_specs=P(None, ("store", "vocab")),
        check_vma=False,
    )
```

time: 171 us -> 62 us (0.36)
  blocking collectives: 81 us -> 0 us
  Pallas kernels: 0 us -> 54.9 us
  waiting for transfers between devices: 32.4 us -> 0 us
  matrix products: 26.6 us -> 0 us
  between operations: 13.4 us -> 0.02 us
  starting transfers between devices: 9.87 us -> 0 us
  other arithmetic: 5.86 us -> 0 us
  local copies, waits for them, and re-layouts: 1.45 us -> 6.85 us
    pallas_call x0 -> x2, Pallas kernels: none -> 54.9 us  [the longest x1 50.3 us: body(): pl.pallas_call(functools.partial(gather_kernel, S, V), out_shape=(jax.Sha...]
    psum x1 -> x0, blocking collectives: 41.6 us -> none  [body(): lax.psum((jnp.sum(lm_terms, axis=1), jnp.sum(kernel, axis=1)), ('store',...]
    pmax x1 -> x0, blocking collectives: 39.4 us -> none  [body(): lax.pmax((jnp.max(logits, axis=1), jnp.max(masked, axis=1)), ('store', 'v...]
    all_gather x1 -> x0, waiting for transfers between devices: 31.7 us -> none  [body(): portion = lax.all_gather(hidden, 'store', axis=0, tiled=True)]
    dot_general x3 -> x0, matrix products: 26.6 us -> none  [the longest x1 17.1 us: body(): logit_rows = jnp.dot(portion, lm_head, preferred_element_type=jnp.float32)]
    all_to_all x2 -> x0, starting transfers between devices: 9.87 us -> none  [the longest x1 6.32 us: body(): lax.all_to_all(values[None, :], 'vocab', split_axis=1, concat_axis=1, til...]
    unnamed x8 -> x12, local copies, waits for them, and re-layouts: 0.02 us -> 6.85 us
    reduce_sum x3 -> x0, other arithmetic: 5.84 us -> none  [the longest x1 2.88 us: body(): jnp.sum(lm_terms, axis=1)]
  transfers between devices with their start and end apart: 3 -> 0, of which waited for: 1 -> 0; matrix products, arithmetic and copies ran while one was open for 14% -> 0% of each run, Pallas kernels for 0% -> 0%
where the time goes in v1:
time: 62 us; the launch traced here: 61.8 us
  Pallas kernels  54.9 us (89%)
  local copies, waits for them, and re-layouts  6.85 us (11%)
    pallas_call x1, Pallas kernels, body(): pl.pallas_call(functools.partial(gather_kernel, S, V), out_shape=(jax.Sha...  50.3 us
    unnamed x12, local copies, waits for them, and re-layouts  6.85 us
    pallas_call x1, Pallas kernels, body(): pl.pallas_call(mixture_kernel, grid=(C // CT,), out_shape=jax.ShapeDtypeS...  4.57 us

profile of v1, /device:TPU:0, one launch (start us, length us, event | category | flops | bytes accessed | tf_op | source)
XLA Modules:
  0.0 61.8 jit_solution(17805987780083025046)
XLA Ops:
  0.0 0.0 copy-start.1
  0.0 1.6 %copy-done.1 = bf16[256,4096]{1,0:T(8,128)(2,1)S(1)} copy-done((bf16[256,4096]{1,0:T(8,128)(2,1)S(1)}, bf16[256,4096]{1,0:T(8,128)(2,1)}, u32[]{:S(2)}) %copy-start.1) | copy-done | bytes 2097176
  1.6 0.0 copy-start.2
  1.6 1.0 %copy-done.2 = bf16[64,4096]{1,0:T(8,128)(2,1)S(1)} copy-done((bf16[64,4096]{1,0:T(8,128)(2,1)S(1)}, bf16[64,4096]{1,0:T(8,128)(2,1)}, u32[]{:S(2)}) %copy-start.2) | copy-done | bytes 524312
  2.6 0.0 copy-start.3
  2.6 0.7 %copy-done.3 = s32[512]{0:T(512)S(1)} copy-done((s32[512]{0:T(512)S(1)}, s32[512]{0:T(512)}, u32[]{:S(2)}) %copy-start.3) | copy-done | bytes 2072
  3.3 0.0 copy-start.4
  3.3 0.7 %copy-done.4 = s32[256]{0:T(256)S(1)} copy-done((s32[256]{0:T(256)S(1)}, s32[256]{0:T(256)}, u32[]{:S(2)}) %copy-start.4) | copy-done | bytes 1048
  4.0 0.0 copy-start.5
  4.0 0.7 %copy-done.5 = s32[256]{0:T(256)S(1)} copy-done((s32[256]{0:T(256)S(1)}, s32[256]{0:T(256)}, u32[]{:S(2)}) %copy-start.5) | copy-done | bytes 1048
  4.7 50.3 %gather_score.1 = (f32[512,2048]{1,0:T(8,128)}, bf16[256,512]{1,0:T(8,128)(2,1)S(1)}, s32[256,128]{1,0:T(8,128)S(1)}, f32[512,128]{1,0:T(8,128)S(1)}) custom-call(bf16[64,4096]{1,0:T(8,128)(2,1)S(1)} %copy-done.2, bf16[4096,2048]{1,0:T(8,128)(2,1)} %lm_head.1, bf16[256,4096]{1,0:T(8,128)(2,1)S(1)} %copy-done.1, s32[1,256]{1,0:T(1,128)S(1)} %bitcast.4, ...), custom_call_target="tpu_custom_call" | custom-call | tf_op jit(solution)/shard_map/gather_score/pallas_call | solution.py:332
  55.0 0.0 copy-start
  55.0 2.2 %copy-done = f32[512,2048]{1,0:T(8,128)S(1)} copy-done((f32[512,2048]{1,0:T(8,128)S(1)}, f32[512,2048]{1,0:T(8,128)}, u32[]{:S(2)}) %copy-start) | copy-done | bytes 4194328
  57.2 4.6 %mixture.1 = f32[512,2048]{1,0:T(8,128)} custom-call(bf16[256,512]{1,0:T(8,128)(2,1)S(1)} %get-tuple-element.9.weights, s32[256,128]{1,0:T(8,128)S(1)} %get-tuple-element.10.tokens, f32[512,128]{1,0:T(8,128)S(1)} %get-tuple-element.11.shift, f32[512,2048]{1,0:T(8,128)S(1)} %copy-done), custom_call_target="tpu_custom_call" | custom-call | tf_op jit(solution)/shard_map/mixture/pallas_call | solution.py:373
Async XLA Ops:
  0.0 1.6 %copy-start.1 = (bf16[256,4096]{1,0:T(8,128)(2,1)S(1)}, bf16[256,4096]{1,0:T(8,128)(2,1)}, u32[]{:S(2)}) copy-start(bf16[256,4096]{1,0:T(8,128)(2,1)} %keys.1) | copy-start | bytes 6291460
  1.6 1.0 %copy-start.2 = (bf16[64,4096]{1,0:T(8,128)(2,1)S(1)}, bf16[64,4096]{1,0:T(8,128)(2,1)}, u32[]{:S(2)}) copy-start(bf16[64,4096]{1,0:T(8,128)(2,1)} %hidden.1) | copy-start | bytes 1572868
  2.6 0.7 %copy-start.3 = (s32[512]{0:T(512)S(1)}, s32[512]{0:T(512)}, u32[]{:S(2)}) copy-start(s32[512]{0:T(512)} %param.11) | copy-start | bytes 6148
  3.3 0.7 %copy-start.4 = (s32[256]{0:T(256)S(1)}, s32[256]{0:T(256)}, u32[]{:S(2)}) copy-start(s32[256]{0:T(256)} %param.9) | copy-start | bytes 3076
  4.0 0.7 %copy-start.5 = (s32[256]{0:T(256)S(1)}, s32[256]{0:T(256)}, u32[]{:S(2)}) copy-start(s32[256]{0:T(256)} %param.10) | copy-start | bytes 3076
  55.0 2.2 %copy-start = (f32[512,2048]{1,0:T(8,128)S(1)}, f32[512,2048]{1,0:T(8,128)}, u32[]{:S(2)}) copy-start(f32[512,2048]{1,0:T(8,128)} %get-tuple-element.12.logits) | copy-start | bytes 12582916

commit v2 on v1

--- a/solution.py
+++ b/solution.py
@@ -9,7 +9,8 @@
 from jax.sharding import PartitionSpec as P
 
 NEG_FILL = -1e30
-DEPTH_CHUNK = 512
+DEPTH_CHUNK = 1024
+COLUMN_CHUNK = 1024
 MESH = pl.DeviceIdType.MESH
 
 
@@ -21,8 +22,8 @@
     S, V,
     hidden, lm_head, keys, values, licences, allowed,
     logits_out, weights_out, tokens_out, shift_out,
-    hid, head, key, logits, scores, half, wsend, wrecv, tok, tokcol, turn, stat, st1, st1_all, st2, st2_all,
-    own_sem, head_sem, key_sem, out_sem, gsend, grecv, tsend, trecv, wsend_sem, wrecv_sem,
+    hid, head, key, lic, allow, val, logits, scores, half, wsend, wrecv, tok, tokcol, turn, stat, st1, st1_all, st2, st2_all,
+    own_sem, head_sem, key_sem, small_sem, out_sem, gsend, grecv, tsend, trecv, wsend_sem, wrecv_sem,
     s1send, s1recv, s2send, s2recv,
 ):
     R, D = hidden.shape
@@ -67,7 +68,12 @@
 
     loop_all(lambda k: own_copy(k).start())
     loop_all(lambda k: key_copy(k).start())
-    tok[...] = jnp.broadcast_to(values[...], tok.shape)
+    small = [
+        pltpu.make_async_copy(src, dst, small_sem.at[i])
+        for i, (src, dst) in enumerate(((values, val), (licences, lic), (allowed, allow)))
+    ]
+    for copy in small:
+        copy.start()
 
     store_peers = [lax.rem(s + j, S) for j in range(1, S)]
     vocab_peers = [lax.rem(v + j, V) for j in range(1, V)]
@@ -124,6 +130,9 @@
             loop_all(lambda k: send(t, k).start())
     loop_all(lambda k: head_copy(k).start())
 
+    for copy in small:
+        copy.wait()
+    tok[...] = jnp.broadcast_to(val[...], tok.shape)
     token_sends = []
     for j in range(1, V):
         copy = remote(tok, tokcol.at[v], tsend.at[j - 1], trecv.at[j - 1], s, vocab_peers[j - 1])
@@ -143,13 +152,15 @@
 
     lax.fori_loop(0, K, norm_step, 0)
 
-    NT = math.gcd(C, 256)
-
-    def compute(k):
+    NT = math.gcd(C, COLUMN_CHUNK)
+
+    def add_scores(k):
         own_copy(k).wait()
         scores[...] += lax.dot_general(
             key[k], hid[k], (((1,), (1,)), ((), ())), preferred_element_type=jnp.float32
         )
+
+    def add_logits(k):
         head_copy(k).wait()
 
         def column_step(n, carry):
@@ -161,8 +172,13 @@
 
         lax.fori_loop(0, C // NT, column_step, 0)
 
-    if tuned:
-        def gather_step(k, carry):
+    def ready(k):
+        for t in range(3, 7) if tuned else range(len(streams)):
+            arrive(t, k).wait_recv()
+        add_scores(k)
+
+    def gather_step(k, carry):
+        if tuned:
             @pl.when(k < K)
             def _():
                 arrive(0, k).wait_recv()
@@ -170,6 +186,7 @@
                 send(2, k).start()
                 send(4, k).start()
 
+        if tuned:
             @pl.when(jnp.logical_and(k >= 1, k <= K))
             def _():
                 arrive(1, k - 1).wait_recv()
@@ -177,31 +194,21 @@
                 arrive(2, k - 1).wait_recv()
                 send(6, k - 1).start()
 
-            @pl.when(k >= 2)
-            def _():
-                for t in range(3, 7):
-                    arrive(t, k - 2).wait_recv()
-                compute(k - 2)
-
-            return carry
-
-        lax.fori_loop(0, K + 2, gather_step, 0)
-    else:
-        def gather_step(k, carry):
-            for t in range(len(streams)):
-                arrive(t, k).wait_recv()
-            compute(k)
-            return carry
-
-        lax.fori_loop(0, K, gather_step, 0)
-
-    out_copy = pltpu.make_async_copy(logits, logits_out, out_sem)
-    out_copy.start()
-
-    licence = row_to_column(licences[...])[:, 0:1]
+        @pl.when(k >= lag)
+        def _():
+            ready(k - lag)
+            add_logits(k - lag)
+
+        return carry
+
+    lag = 2 if tuned else 0
+    lax.fori_loop(0, K - 1 + lag, gather_step, 0)
+    ready(K - 1)
+
+    licence = row_to_column(lic[...])[:, 0:1]
     permitted = jnp.bitwise_and(
         jnp.right_shift(
-            jnp.broadcast_to(allowed[...], (E, Q)), jnp.broadcast_to(licence, (E, Q))
+            jnp.broadcast_to(allow[...], (E, Q)), jnp.broadcast_to(licence, (E, Q))
         ), 1) == 1
     masked = jnp.where(
         permitted, scores[...] * inverse_root - (0.5 * inverse_root) * half[...], NEG_FILL
@@ -221,6 +228,9 @@
         weight_sends.append(copy)
     wrecv[v] = wsend[pl.ds(pl.multiple_of(v * B, B), B), :]
 
+    add_logits(K - 1)
+    out_copy = pltpu.make_async_copy(logits, logits_out, out_sem)
+    out_copy.start()
     RT = math.gcd(Q, 64)
     lane = lax.broadcasted_iota(jnp.int32, (RT, 128), 1)
 
@@ -312,8 +322,9 @@
         weights[...], table, (((0,), (0,)), ((), ())), preferred_element_type=jnp.float32
     )
     ours = logits[...] - shift[:, 0:1]
-    theirs = jnp.where(share > 0.0, jnp.log(jnp.where(share > 0.0, share, 1.0)), -jnp.inf)
-    out[...] = jnp.maximum(ours, theirs) + jnp.log(1.0 + jnp.exp(-jnp.abs(ours - theirs)))
+    base = jnp.maximum(ours, -80.0)
+    both = base + jnp.log(jnp.exp(ours - base) + share * jnp.exp(-base))
+    out[...] = jnp.where(share > 0.0, both, ours)
 
 
 def body(S, V, hidden, lm_head, keys, values, licences, allowed):
@@ -325,7 +336,7 @@
     KC = math.gcd(D, DEPTH_CHUNK)
     K = D // KC
     streams = S - 1
-    any_space = pl.BlockSpec(memory_space=pl.ANY)
+    hbm = pl.BlockSpec(memory_space=pltpu.HBM)
     vmem = pl.BlockSpec(memory_space=pltpu.VMEM)
     f32 = jnp.float32
     dma = pltpu.SemaphoreType.DMA
@@ -337,12 +348,15 @@
             jax.ShapeDtypeStruct((E, 128), jnp.int32),
             jax.ShapeDtypeStruct((Q, 128), f32),
         ),
-        in_specs=[any_space] * 3 + [vmem] * 3,
-        out_specs=(any_space, vmem, vmem, vmem),
+        in_specs=[hbm] * 6,
+        out_specs=(hbm, vmem, vmem, vmem),
         scratch_shapes=[
             pltpu.VMEM((K, Q, KC), hidden.dtype),
             pltpu.VMEM((K, KC, C), lm_head.dtype),
             pltpu.VMEM((K, E, KC), keys.dtype),
+            pltpu.VMEM((1, E), jnp.int32),
+            pltpu.VMEM((1, Q), jnp.int32),
+            pltpu.VMEM((1, E), jnp.int32),
             pltpu.VMEM((Q, C), f32),
             pltpu.VMEM((E, Q), f32),
             pltpu.VMEM((E, 1), f32),
@@ -356,18 +370,18 @@
             pltpu.VMEM((S, 8, Q), f32),
             pltpu.VMEM((8, Q), f32),
             pltpu.VMEM((V, 8, Q), f32),
-            dma((K,)), dma((K,)), dma((K,)), dma(()),
+            dma((K,)), dma((K,)), dma((K,)), dma((3,)), dma(()),
             dma((streams, K)), dma((streams, K)),
             dma((V - 1,)), dma((V - 1,)), dma((V - 1,)), dma((V - 1,)),
             dma((S - 1,)), dma((S - 1,)), dma((V - 1,)), dma((V - 1,)),
         ],
         compiler_params=pltpu.CompilerParams(
-            collective_id=0, has_side_effects=True, vmem_limit_bytes=48 * 1024 * 1024
+            collective_id=0, has_side_effects=True, vmem_limit_bytes=60 * 1024 * 1024
         ),
         name="gather_score",
     )(hidden, lm_head, keys, values.reshape(1, E), licences.reshape(1, E), allowed.reshape(1, Q))
 
-    CT = math.gcd(C, 512)
+    CT = math.gcd(C, COLUMN_CHUNK)
     fixed = lambda shape: pl.BlockSpec(shape, lambda n: (0, 0))
     tile = pl.BlockSpec((Q, CT), lambda n: (0, n))
     return pl.pallas_call(
@@ -376,7 +390,7 @@
         out_shape=jax.ShapeDtypeStruct((Q, C), f32),
         in_specs=[fixed((E, Q)), fixed((E, 128)), fixed((Q, 128)), tile],
         out_specs=tile,
-        compiler_params=pltpu.CompilerParams(vmem_limit_bytes=48 * 1024 * 1024),
+        compiler_params=pltpu.CompilerParams(vmem_limit_bytes=60 * 1024 * 1024),
         name="mixture",
     )(weights, tokens, shift, logits)
 

time: 62 us -> 48.9 us (0.79)
  local copies, waits for them, and re-layouts: 6.85 us -> 0 us
  Pallas kernels: 54.9 us -> 48.8 us
    pallas_call x1, Pallas kernels: 50.3 us -> 43.2 us  [body(): pl.pallas_call(functools.partial(gather_kernel, S, V), out_shape=(jax.Sha...]
    unnamed x12 -> x0, local copies, waits for them, and re-layouts: 6.85 us -> none
    pallas_call x1, Pallas kernels: 4.57 us -> 5.56 us  [body(): pl.pallas_call(mixture_kernel, grid=(C // CT,), out_shape=jax.ShapeDtypeS...]
where the time goes in v2:
time: 48.9 us; the launch traced here: 48.8 us
  Pallas kernels  48.8 us (100%)
    pallas_call x1, Pallas kernels, body(): pl.pallas_call(functools.partial(gather_kernel, S, V), out_shape=(jax.Sha...  43.2 us
    pallas_call x1, Pallas kernels, body(): pl.pallas_call(mixture_kernel, grid=(C // CT,), out_shape=jax.ShapeDtypeS...  5.56 us

profile of v2, /device:TPU:0, one launch (start us, length us, event | category | flops | bytes accessed | tf_op | source)
XLA Modules:
  0.0 48.8 jit_solution(10821842609302495755)
XLA Ops:
  0.0 43.2 %gather_score.1 = (f32[512,2048]{1,0:T(8,128)}, bf16[256,512]{1,0:T(8,128)(2,1)}, s32[256,128]{1,0:T(8,128)}, f32[512,128]{1,0:T(8,128)}) custom-call(bf16[64,4096]{1,0:T(8,128)(2,1)} %hidden.1, bf16[4096,2048]{1,0:T(8,128)(2,1)} %lm_head.1, bf16[256,4096]{1,0:T(8,128)(2,1)} %keys.1, s32[1,256]{1,0:T(1,128)} %bitcast.4, s32[1,256]{1,0:T(1,128)} %bitcast.5, ...), custom_call_target="tpu_custom_call" | custom-call | tf_op jit(solution)/shard_map/gather_score/pallas_call | solution.py:343
  43.2 5.6 %mixture.1 = f32[512,2048]{1,0:T(8,128)} custom-call(bf16[256,512]{1,0:T(8,128)(2,1)} %get-tuple-element.9.weights, s32[256,128]{1,0:T(8,128)} %get-tuple-element.10.tokens, f32[512,128]{1,0:T(8,128)} %get-tuple-element.11.shift, f32[512,2048]{1,0:T(8,128)} %get-tuple-element.12.logits), custom_call_target="tpu_custom_call" | custom-call | tf_op jit(solution)/shard_map/mixture/pallas_call | solution.py:387

commit v3 on v2

--- a/solution.py
+++ b/solution.py
@@ -111,10 +111,7 @@
 
     def send(t, k):
         origin, target, _ = streams[t]
-        if origin is s:
-            src = hidden.at[:, pl.ds(pl.multiple_of(k * KC, KC), KC)]
-        else:
-            src = hid.at[k, rows(origin)]
+        src = hid.at[k, rows(origin)]
         return remote(src, hid.at[k, rows(origin)], gsend.at[t, k], grecv.at[t, k], *target)
 
     def arrive(t, k):
@@ -123,9 +120,13 @@
         return remote(block, block, gsend.at[t, k], grecv.at[t, k], *target)
 
     if tuned:
-        loop_all(lambda k: send(0, k).start())
-        loop_all(lambda k: send(3, k).start())
+        def begin(k):
+            own_copy(k).wait()
+            send(0, k).start()
+            send(3, k).start()
+        loop_all(begin)
     else:
+        loop_all(lambda k: own_copy(k).wait())
         for t in range(len(streams)):
             loop_all(lambda k: send(t, k).start())
     loop_all(lambda k: head_copy(k).start())
@@ -152,10 +153,9 @@
 
     lax.fori_loop(0, K, norm_step, 0)
 
-    NT = math.gcd(C, COLUMN_CHUNK)
+    NT = math.gcd(C, 2 * COLUMN_CHUNK)
 
     def add_scores(k):
-        own_copy(k).wait()
         scores[...] += lax.dot_general(
             key[k], hid[k], (((1,), (1,)), ((), ())), preferred_element_type=jnp.float32
         )

time: 48.9 us -> 48.2 us (0.986)
  Pallas kernels: 48.8 us -> 48 us
    pallas_call x1, Pallas kernels: 43.2 us -> 42.5 us  [body(): pl.pallas_call(functools.partial(gather_kernel, S, V), out_shape=(jax.Sha...]
where the time goes in v3:
time: 48.2 us; the launch traced here: 48 us
  Pallas kernels  48 us (100%)
    pallas_call x1, Pallas kernels, body(): pl.pallas_call(functools.partial(gather_kernel, S, V), out_shape=(jax.Sha...  42.5 us
    pallas_call x1, Pallas kernels, body(): pl.pallas_call(mixture_kernel, grid=(C // CT,), out_shape=jax.ShapeDtypeS...  5.56 us

profile of v3, /device:TPU:0, one launch (start us, length us, event | category | flops | bytes accessed | tf_op | source)
XLA Modules:
  0.0 48.0 jit_solution(14978153149298013516)
XLA Ops:
  0.0 42.5 %gather_score.1 = (f32[512,2048]{1,0:T(8,128)}, bf16[256,512]{1,0:T(8,128)(2,1)}, s32[256,128]{1,0:T(8,128)}, f32[512,128]{1,0:T(8,128)}) custom-call(bf16[64,4096]{1,0:T(8,128)(2,1)} %hidden.1, bf16[4096,2048]{1,0:T(8,128)(2,1)} %lm_head.1, bf16[256,4096]{1,0:T(8,128)(2,1)} %keys.1, s32[1,256]{1,0:T(1,128)} %bitcast.4, s32[1,256]{1,0:T(1,128)} %bitcast.5, ...), custom_call_target="tpu_custom_call" | custom-call | tf_op jit(solution)/shard_map/gather_score/pallas_call | solution.py:343
  42.5 5.6 %mixture.1 = f32[512,2048]{1,0:T(8,128)} custom-call(bf16[256,512]{1,0:T(8,128)(2,1)} %get-tuple-element.9.weights, s32[256,128]{1,0:T(8,128)} %get-tuple-element.10.tokens, f32[512,128]{1,0:T(8,128)} %get-tuple-element.11.shift, f32[512,2048]{1,0:T(8,128)} %get-tuple-element.12.logits), custom_call_target="tpu_custom_call" | custom-call | tf_op jit(solution)/shard_map/mixture/pallas_call | solution.py:387

commit v4 on v3

--- a/solution.py
+++ b/solution.py
@@ -231,7 +231,7 @@
     add_logits(K - 1)
     out_copy = pltpu.make_async_copy(logits, logits_out, out_sem)
     out_copy.start()
-    RT = math.gcd(Q, 64)
+    RT = math.gcd(Q, 128)
     lane = lax.broadcasted_iota(jnp.int32, (RT, 128), 1)
 
     def stat_step(r, carry):

time: 48.2 us -> 47.5 us (0.985)
  Pallas kernels: 48 us -> 47.3 us
    pallas_call x1, Pallas kernels: 42.5 us -> 41.8 us  [body(): pl.pallas_call(functools.partial(gather_kernel, S, V), out_shape=(jax.Sha...]
where the time goes in v4:
time: 47.5 us; the launch traced here: 47.3 us
  Pallas kernels  47.3 us (100%)
    pallas_call x1, Pallas kernels, body(): pl.pallas_call(functools.partial(gather_kernel, S, V), out_shape=(jax.Sha...  41.8 us
    pallas_call x1, Pallas kernels, body(): pl.pallas_call(mixture_kernel, grid=(C // CT,), out_shape=jax.ShapeDtypeS...  5.55 us

profile of v4, /device:TPU:0, one launch (start us, length us, event | category | flops | bytes accessed | tf_op | source)
XLA Modules:
  0.0 47.3 jit_solution(18113345767181781383)
XLA Ops:
  0.0 41.8 %gather_score.1 = (f32[512,2048]{1,0:T(8,128)}, bf16[256,512]{1,0:T(8,128)(2,1)}, s32[256,128]{1,0:T(8,128)}, f32[512,128]{1,0:T(8,128)}) custom-call(bf16[64,4096]{1,0:T(8,128)(2,1)} %hidden.1, bf16[4096,2048]{1,0:T(8,128)(2,1)} %lm_head.1, bf16[256,4096]{1,0:T(8,128)(2,1)} %keys.1, s32[1,256]{1,0:T(1,128)} %bitcast.4, s32[1,256]{1,0:T(1,128)} %bitcast.5, ...), custom_call_target="tpu_custom_call" | custom-call | tf_op jit(solution)/shard_map/gather_score/pallas_call | solution.py:343
  41.8 5.6 %mixture.1 = f32[512,2048]{1,0:T(8,128)} custom-call(bf16[256,512]{1,0:T(8,128)(2,1)} %get-tuple-element.9.weights, s32[256,128]{1,0:T(8,128)} %get-tuple-element.10.tokens, f32[512,128]{1,0:T(8,128)} %get-tuple-element.11.shift, f32[512,2048]{1,0:T(8,128)} %get-tuple-element.12.logits), custom_call_target="tpu_custom_call" | custom-call | tf_op jit(solution)/shard_map/mixture/pallas_call | solution.py:387
